TPU v7x, 512 devices: a whole 4x4x16 slice. The times are simulated.
512 devices in a mesh: layer: 8 (over y, core), latent: 64 (over x, z).
Axes of the slice: x: 4, y: 4, z: 16, core: 2. Of those that a mesh axis runs over, the one named last changes fastest.
Arguments:
- resid: bfloat16 [4, 128, 3584], P(None, 'latent'), may hold values from -6 to 6
- target: bfloat16 [5, 128, 3584], P(None, 'latent'), may hold values from -6 to 6
- enc_weight: bfloat16 [8, 3584, 8192], P('layer', None, 'latent'), may hold values from -0.09375 to 0.09375
- enc_bias: float32 [8, 8192], P('layer', 'latent'), may hold values from -3 to 3
- dec_weight: bfloat16 [8, 2, 2, 8192, 1792], P('layer', None, None, 'latent'), may hold values from -0.046875 to 0.046875
- blocks: int32 [4, 1, 96], replicated, may hold values from 0 to 127, all different within a row
Outputs:
- errors: bfloat16 [8, 128, 1792], P('layer', 'latent')
- enc_grad: bfloat16 [8, 3584, 8192], P('layer', None, 'latent')
- bias_grad: float32 [8, 8192], P('layer', 'latent')
Inputs may be any that keep to these rules, and one draw needn't show every extreme that they name: Each row names 96 different blocks; every block is named in some row.
All inputs are finite; a program needn't handle non-finite values.
Results may differ from a plain program's by a relative error of at most 0.007.
Values may be sent and summed in bfloat16 or wider, within the bound.
A program may use at most 64 MiB of HBM per device.

v0:
```python
import jax
import jax.numpy as jnp
from jax import lax
from jax.sharding import Mesh
from jax.sharding import PartitionSpec as P

LATENT = ("latent_0", "latent_1")


def laid_out(pieces, dim):
    pieces = jnp.moveaxis(pieces, 0, dim)
    shape = pieces.shape
    return pieces.reshape(*shape[:dim], shape[dim] * shape[dim + 1], *shape[dim + 2 :])


def all_blocks(shard, axes, sequence):
    pieces = shard[None]
    for k in sequence:
        pieces = lax.all_gather(pieces, axes[k], axis=0, tiled=True)
    held = [lax.axis_size(axes[k]) for k in reversed(sequence)]
    pieces = pieces.reshape(*held, *shard.shape)
    turned = sorted(range(len(sequence)), key=lambda place: sequence[len(sequence) - 1 - place])
    return pieces.transpose(*turned, *range(len(sequence), pieces.ndim)).reshape(-1, *shard.shape)


def gathered_by_axis(shard, axes, sequence, dim):
    return laid_out(all_blocks(shard, axes, sequence), dim)


def swapped(shard, axis, stride):
    return lax.ppermute(shard, axis, [(i, i ^ 1 << stride) for i in range(lax.axis_size(axis))])


def split_up(shard, dim, count):
    shape = shard.shape
    pieces = shard.reshape(*shape[:dim], count, shape[dim] // count, *shape[dim + 1 :])
    return jnp.moveaxis(pieces, dim, 0)


def sent_and_summed(shard, axis, dim):
    count = lax.axis_size(axis)
    pieces = lax.all_to_all(split_up(shard, dim, count), axis, 0, 0, tiled=True)
    return jnp.sum(pieces, axis=0)


def summed_rows(shard, axes, dim):
    far, near = axes
    return sent_and_summed(sent_and_summed(shard, far, dim), near, dim)


def from_behind(block, axis, distance):
    devices = range(lax.axis_size(axis))
    route = [(i - distance, i) for i in devices if i - distance in devices]
    return lax.ppermute(block, axis, route)


def sent_to_all(shard, axis):
    count = lax.axis_size(axis)
    return lax.all_to_all(
        jnp.broadcast_to(shard[None], (count, *shard.shape)), axis, 0, 0, tiled=True
    )


def gathered_copies(shard, axis, dim):
    return laid_out(sent_to_all(shard, axis), dim)


def in_one_piece(arrays, axis, dim, along):
    ends, at = ([], 0)
    for a in arrays[:-1]:
        at += a.shape[along]
        ends.append(at)
    both = jnp.concatenate(arrays, axis=along)
    return tuple(jnp.split(gathered_copies(both, axis, dim), ends, axis=along))


def contract_rows(left_rows, right_rows):
    return lax.dot_general(
        left_rows, right_rows, (((0,), (0,)), ((), ())), preferred_element_type=jnp.float32
    )


def contract_cols(left_rows, right_rows):
    return lax.dot_general(
        left_rows, right_rows, (((1,), (1,)), ((), ())), preferred_element_type=jnp.float32
    )


def on_device(resid, target, enc_weight, enc_bias, dec_weight, blocks):
    latent_devices = lax.axis_size(LATENT)
    layer_slot = lax.axis_index("layer")
    layer_row = layer_slot // 2
    which_half = layer_slot % 2
    column_pos = lax.axis_index(LATENT)
    rows_in = lax.dynamic_index_in_dim(resid, layer_row, 0, keepdims=False)
    local_rows = rows_in.shape[0]
    token_count = local_rows * latent_devices
    weight_in = enc_weight[0]
    block_width = weight_in.shape[1]
    decoder = dec_weight[0]
    column_width = decoder.shape[-1]
    dec_own = decoder[0].reshape(2 * block_width, column_width)
    dec_next = decoder[1].reshape(2 * block_width, column_width)
    listed = lax.dynamic_index_in_dim(blocks, layer_row, 0, keepdims=False)
    tile_len = token_count // listed.shape[0]
    flags = jnp.any(listed == which_half * latent_devices + column_pos, axis=1).astype(jnp.float32)
    gate_mask = jnp.repeat(flags, tile_len)[:, None]
    whole_in = gathered_by_axis(rows_in, LATENT, (0, 1), 0)
    preact = jnp.dot(whole_in, weight_in, preferred_element_type=jnp.float32)
    preact = preact + enc_bias[0][None, :]
    latents_on = (preact * gate_mask).astype(jnp.bfloat16)
    partner = swapped(latents_on, "layer", 0)
    lower_half = jnp.where(which_half == 0, latents_on, partner)
    upper_half = jnp.where(which_half == 0, partner, latents_on)
    pair_acts = jnp.concatenate([lower_half, upper_half], axis=1)
    totals = summed_rows(
        jnp.concatenate(
            [
                jnp.dot(pair_acts, dec_own, preferred_element_type=jnp.float32),
                jnp.dot(pair_acts, dec_next, preferred_element_type=jnp.float32),
            ],
            axis=1,
        ),
        ("latent_0", "latent_1"),
        0,
    )
    own_sum = totals[:, :column_width]
    ahead_part = totals[:, column_width:]
    targets = lax.dynamic_slice_in_dim(target, layer_row, 2, 0)
    targets = lax.dynamic_slice_in_dim(targets, which_half * column_width, column_width, 2).astype(
        jnp.float32
    )
    behind = from_behind(ahead_part, "layer", 2)
    err_own = (own_sum + behind - targets[0]).astype(jnp.bfloat16)
    next_own = from_behind(own_sum, "layer", -2)
    err_next = (next_own + ahead_part - targets[1]).astype(jnp.bfloat16)
    piece_pair = in_one_piece((err_own, err_next), LATENT, 0, 1)
    grad_pair = contract_cols(piece_pair[0], dec_own) + contract_cols(piece_pair[1], dec_next)
    lower_grad = grad_pair[:, :block_width]
    upper_grad = grad_pair[:, block_width:]
    own_part = jnp.where(which_half == 0, lower_grad, upper_grad)
    their_part = jnp.where(which_half == 0, upper_grad, lower_grad)
    received = swapped(their_part, "layer", 0)
    grad_pre = (own_part + received) * gate_mask
    bias_grad = jnp.sum(grad_pre, axis=0)[None, :]
    grad_low = grad_pre.astype(jnp.bfloat16)
    grad_weight = contract_rows(whole_in, grad_low)
    return (err_own[None], grad_weight.astype(jnp.bfloat16)[None], bias_grad)


def solution(mesh):
    finer = Mesh(
        mesh.devices.reshape(mesh.shape["layer"], 4, 16), ("layer", "latent_0", "latent_1")
    )
    placed = (
        P(None, LATENT, None),
        P(None, LATENT, None),
        P("layer", None, LATENT),
        P("layer", LATENT),
        P("layer", None, None, LATENT, None),
        P(),
    )
    return jax.shard_map(
        on_device,
        mesh=finer,
        in_specs=placed,
        out_specs=(P("layer", LATENT, None), P("layer", None, LATENT), P("layer", LATENT)),
        check_vma=False,
    )
```

profile of v0, /device:TPU:1, one launch (start us, length us, event | category | flops | bytes accessed | tf_op | source)
XLA Modules:
  0.0 202.1 jit_solution(11026004268313117025)
XLA Ops:
  0.6 0.0 copy-start
  0.7 0.8 constant_dynamic-slice_fusion.1
  1.5 10.2 %all_gather.6 = bf16[4,2,3584]{2,1,0:T(2,128)(2,1)S(1)} all-gather(bf16[1,2,3584]{2,1,0:T(2,128)(2,1)S(1)} %constant_dynamic-slice_fusion.1), channel_id=1, replica_groups=mesh['layer'=8,'latent_0'=4,'latent_1'=16] {'latent_0'}, dimensions={0}, use_global_device_ids=true | all-gather | bytes 71680 | tf_op jit(solution)/shard_map/all_gather | solution.py:19
  11.6 34.1 %all_gather.7 = bf16[64,2,3584]{2,1,0:T(2,128)(2,1)S(1)} all-gather(bf16[4,2,3584]{2,1,0:T(2,128)(2,1)S(1)} %all_gather.6), channel_id=1, replica_groups=mesh['layer'=8,'latent_0'=4,'latent_1'=16] {'latent_1'}, dimensions={0}, use_global_device_ids=true | all-gather | bytes 974848 | tf_op jit(solution)/shard_map/all_gather | solution.py:19
  45.7 0.0 copy-start.3
  45.7 0.6 copy.30
  46.4 0.3 reshape_reshape.3
  46.7 1.3 compare_reduce_fusion
  48.7 0.0 copy-start.1
  48.7 0.0 copy-done
  48.7 0.0 copy-done.3
  48.7 0.5 fusion.2
  49.2 12.2 %collective-permute-start = (bf16[128,128]{0,1:T(8,128)(2,1)S(1)}, bf16[128,128]{0,1:T(8,128)(2,1)S(1)}, u32[]{:S(2)}, u32[]{:S(2)}) collective-permute-start(bf16[128,128]{0,1:T(8,128)(2,1)S(1)} %fusion.2), channel_id=1, source_target_pairs={{0,64},{64,0},{128,192},{192,128},{256,320},{320,256},{384,448},{4... | collective-permute-start | bytes 98312 | tf_op jit(solution)/shard_map/ppermute | solution.py:31
  61.3 0.0 copy-done.1
  61.4 1.0 fusion.17
  62.4 0.0 collective-permute-done
  62.4 1.5 fusion.8
  63.9 0.3 fusion.7
  64.2 0.2 pad_maximum_fusion
  64.4 26.5 %all_to_all.15 = f32[4,32,3584]{2,1,0:T(8,128)} all-to-all(f32[4,32,3584]{2,1,0:T(8,128)S(1)} %bitcast.38), channel_id=1, replica_groups=mesh['layer'=8,'latent_0'=4,'latent_1'=16] {'latent_0'}, dimensions={0} | all-to-all | bytes 3670016 | tf_op jit(solution)/shard_map/all_to_all | solution.py:42
  91.0 1.6 reduce_sum.27
  92.6 1.0 reshape.43
  93.6 6.7 %all-to-all-start.1 = ((f32[16,2,3584]{2,1,0:T(2,128)}), f32[16,2,3584]{2,1,0:T(2,128)S(1)}, u32[]{:S(2)}, u32[]{:S(2)}) async-start(f32[16,2,3584]{2,1,0:T(2,128)} %reshape.43), calls=%async_computation.1 | async-start | bytes 917504 | tf_op jit(solution)/shard_map/all_to_all | solution.py:42
  100.4 20.8 %all-to-all-done.1 = f32[16,2,3584]{2,1,0:T(2,128)S(1)} async-done(((f32[16,2,3584]{2,1,0:T(2,128)}), f32[16,2,3584]{2,1,0:T(2,128)S(1)}, u32[]{:S(2)}, u32[]{:S(2)}) %all-to-all-start.1) | async-done | bytes 458784 | tf_op jit(solution)/shard_map/all_to_all | solution.py:42
  121.3 0.1 reduce_sum.28
  121.4 3.2 %collective-permute-start.1 = (f32[2,1792]{1,0:T(2,128)S(1)}, f32[2,1792]{1,0:T(2,128)S(1)}, u32[]{:S(2)}, u32[]{:S(2)}) collective-permute-start(f32[2,1792]{1,0:T(2,128)S(1)} %get-tuple-element.12), channel_id=1, source_target_pairs={{0,128},{64,192},{128,256},{192,320},{256,384},{320,448},{1,129},{... | collective-permute-start | bytes 43016 | tf_op jit(solution)/shard_map/ppermute | solution.py:54
  124.6 1.3 collective-permute-start.2
  125.9 0.8 dynamic-slice_convert_fusion
  126.7 0.0 collective-permute-done.1
  126.7 2.3 %collective-permute-done.2 = f32[2,1792]{1,0:T(2,128)S(1)} collective-permute-done((f32[2,1792]{1,0:T(2,128)S(1)}, f32[2,1792]{1,0:T(2,128)S(1)}, u32[]{:S(2)}, u32[]{:S(2)}) %collective-permute-start.2) | collective-permute-done | bytes 14368 | tf_op jit(solution)/shard_map/ppermute | solution.py:54
  129.1 0.0 copy-start.2
  129.1 0.5 broadcast_in_dim.18
  129.6 56.9 %all_to_all.16 = bf16[64,2,3584]{2,1,0:T(2,128)(2,1)} all-to-all(bf16[64,2,3584]{2,1,0:T(2,128)(2,1)S(1)} %broadcast_in_dim.18), channel_id=1, replica_groups=mesh['layer'=8,'latent_0'=4,'latent_1'=16] {'latent_0','latent_1'}, dimensions={0} | all-to-all | bytes 1835008 | tf_op jit(solution)/shard_map/all_to_all | solution.py:59
  186.5 3.2 %reshape.44 = bf16[128,3584]{1,0:T(8,128)(2,1)} reshape(bf16[64,2,3584]{2,1,0:T(2,128)(2,1)} %all_to_all.16) | data formatting | bytes 1835008 | tf_op jit(solution)/shard_map/reshape | solution.py:13
  189.7 0.0 copy-done.2
  189.7 1.7 fusion.5
  191.4 1.4 convolution_add_fusion
  192.8 6.4 %collective-permute-start.3 = (f32[128,128]{0,1:T(8,128)S(1)}, f32[128,128]{0,1:T(8,128)S(1)}, u32[]{:S(2)}, u32[]{:S(2)}) collective-permute-start(f32[128,128]{0,1:T(8,128)S(1)} %slice_select_fusion), channel_id=1, source_target_pairs={{0,64},{64,0},{128,192},{192,128},{256,320},{320,256},{384,448},{4... | collective-permute-start | bytes 196616 | tf_op jit(solution)/shard_map/ppermute | solution.py:31
  199.3 0.9 collective-permute-done.3
  200.2 0.6 fusion.16
  200.8 1.4 fusion
  (5 shorter events, 0.1 us)
Async XLA Ops:
  0.6 48.1 %copy-start = (bf16[1,3584,128]{2,1,0:T(8,128)(2,1)S(1)}, bf16[1,3584,128]{2,1,0:T(8,128)(2,1)}, u32[]{:S(2)}) copy-start(bf16[1,3584,128]{2,1,0:T(8,128)(2,1)} %param.8) | copy-start | bytes 2752516
  45.7 3.0 %copy-start.3 = (f32[1,128]{1,0:T(1,128)S(1)}, f32[1,128]{1,0:T(1,128)}, u32[]{:S(2)}) copy-start(f32[1,128]{1,0:T(1,128)} %param.9) | copy-start | bytes 1540
  48.7 12.7 %copy-start.1 = (bf16[1,2,2,128,1792]{4,3,2,1,0:T(8,128)(2,1)S(1)}, bf16[1,2,2,128,1792]{4,3,2,1,0:T(8,128)(2,1)}, u32[]{:S(2)}) copy-start(bf16[1,2,2,128,1792]{4,3,2,1,0:T(8,128)(2,1)} %param.10) | copy-start | bytes 5505028
  49.2 13.2 %collective-permute-start = (bf16[128,128]{0,1:T(8,128)(2,1)S(1)}, bf16[128,128]{0,1:T(8,128)(2,1)S(1)}, u32[]{:S(2)}, u32[]{:S(2)}) collective-permute-start(bf16[128,128]{0,1:T(8,128)(2,1)S(1)} %fusion.2), channel_id=1, source_target_pairs={{0,64},{64,0},{128,192},{192,128},{256,320},{320,256},{384,448},{4... | collective-permute-start | bytes 98312 | tf_op jit(solution)/shard_map/ppermute | solution.py:31
  93.6 27.6 %all-to-all-start.1 = ((f32[16,2,3584]{2,1,0:T(2,128)}), f32[16,2,3584]{2,1,0:T(2,128)S(1)}, u32[]{:S(2)}, u32[]{:S(2)}) async-start(f32[16,2,3584]{2,1,0:T(2,128)} %reshape.43), calls=%async_computation.1 | async-start | bytes 917504 | tf_op jit(solution)/shard_map/all_to_all | solution.py:42
  121.4 5.3 %collective-permute-start.1 = (f32[2,1792]{1,0:T(2,128)S(1)}, f32[2,1792]{1,0:T(2,128)S(1)}, u32[]{:S(2)}, u32[]{:S(2)}) collective-permute-start(f32[2,1792]{1,0:T(2,128)S(1)} %get-tuple-element.12), channel_id=1, source_target_pairs={{0,128},{64,192},{128,256},{192,320},{256,384},{320,448},{1,129},{... | collective-permute-start | bytes 43016 | tf_op jit(solution)/shard_map/ppermute | solution.py:54
  124.6 4.5 %collective-permute-start.2 = (f32[2,1792]{1,0:T(2,128)S(1)}, f32[2,1792]{1,0:T(2,128)S(1)}, u32[]{:S(2)}, u32[]{:S(2)}) collective-permute-start(f32[2,1792]{1,0:T(2,128)S(1)} %get-tuple-element.11), channel_id=1, source_target_pairs={{128,0},{192,64},{256,128},{320,192},{384,256},{448,320},{129,1},{... | collective-permute-start | bytes 43016 | tf_op jit(solution)/shard_map/ppermute | solution.py:54
  129.1 60.6 %copy-start.2 = (bf16[2,1792]{1,0:T(2,128)(2,1)}, bf16[2,1792]{1,0:T(2,128)(2,1)S(1)}, u32[]{:S(2)}) copy-start(bf16[2,1792]{1,0:T(2,128)(2,1)S(1)} %get-tuple-element.10) | copy-start | bytes 21508
  192.8 7.3 %collective-permute-start.3 = (f32[128,128]{0,1:T(8,128)S(1)}, f32[128,128]{0,1:T(8,128)S(1)}, u32[]{:S(2)}, u32[]{:S(2)}) collective-permute-start(f32[128,128]{0,1:T(8,128)S(1)} %slice_select_fusion), channel_id=1, source_target_pairs={{0,64},{64,0},{128,192},{192,128},{256,320},{320,256},{384,448},{4... | collective-permute-start | bytes 196616 | tf_op jit(solution)/shard_map/ppermute | solution.py:31
where the time goes:
time: 203 us; the launch traced here: 202 us
  blocking collectives  128 us (63%)
  starting transfers between devices  29.8 us (15%)
  waiting for transfers between devices  24.1 us (12%)
  local copies, waits for them, and re-layouts  7.57 us (4%)
  matrix products  6.75 us (3%)
  other arithmetic  4.76 us (2%)
    all_to_all x1, blocking collectives, sent_to_all(): lax.all_to_all(jnp.broadcast_to(shard[None], (count, *shard.shape)), axis...  56.9 us
    all_gather x2, blocking collectives, all_blocks(): pieces = lax.all_gather(pieces, axes[k], axis=0, tiled=True)  44.3 us
    all_to_all x1, blocking collectives, sent_and_summed(): pieces = lax.all_to_all(split_up(shard, dim, count), axis, 0, 0, tiled=True)  26.5 us
    all_to_all x1, waiting for transfers between devices, sent_and_summed(): pieces = lax.all_to_all(split_up(shard, dim, count), axis, 0, 0, tiled=True)  20.8 us
    ppermute x2, starting transfers between devices, swapped(): lax.ppermute(shard, axis, [(i, i ^ 1 << stride) for i in range(lax.axis_s...  18.6 us
    all_to_all x1, starting transfers between devices, sent_and_summed(): pieces = lax.all_to_all(split_up(shard, dim, count), axis, 0, 0, tiled=True)  6.74 us
    ppermute x2, starting transfers between devices, from_behind(): return lax.ppermute(block, axis, route)  4.47 us
  transfers between devices with their start and end apart: 5, of which 3 were waited for; matrix products, arithmetic and copies ran while one was open for 1% of the time, Pallas kernels for 0%

commit v1 on v0

--- a/solution.py
+++ b/solution.py
@@ -16,7 +16,9 @@
 def all_blocks(shard, axes, sequence):
     pieces = shard[None]
     for k in sequence:
-        pieces = lax.all_gather(pieces, axes[k], axis=0, tiled=True)
+        pieces = jnp.concatenate(
+            lax.all_to_all(jnp.stack([pieces] * lax.axis_size(axes[k])), axes[k], 0, 0), axis=0
+        )
     held = [lax.axis_size(axes[k]) for k in reversed(sequence)]
     pieces = pieces.reshape(*held, *shard.shape)
     turned = sorted(range(len(sequence)), key=lambda place: sequence[len(sequence) - 1 - place])

time: 203 us -> 218 us (1.074)
  waiting for transfers between devices: 24.1 us -> 62.4 us
  blocking collectives: 128 us -> 92.3 us
  starting transfers between devices: 29.8 us -> 40.6 us
    all_gather x2 -> x0, blocking collectives: 44.3 us -> none  [all_blocks(): pieces = lax.all_gather(pieces, axes[k], axis=0, tiled=True)]
    all_to_all x0 -> x1, waiting for transfers between devices: none -> 38.2 us  [all_blocks(): lax.all_to_all(jnp.stack([pieces] * lax.axis_size(axes[k])), axes[k], 0, 0)]
    all_to_all x0 -> x1, starting transfers between devices: none -> 14.9 us  [all_blocks(): lax.all_to_all(jnp.stack([pieces] * lax.axis_size(axes[k])), axes[k], 0, 0)]
    all_to_all x0 -> x1, blocking collectives: none -> 9.06 us  [all_blocks(): lax.all_to_all(jnp.stack([pieces] * lax.axis_size(axes[k])), axes[k], 0, 0)]
    ppermute x2, starting transfers between devices: 18.6 us -> 12.8 us  [swapped(): lax.ppermute(shard, axis, [(i, i ^ 1 << stride) for i in range(lax.axis_s...]
  transfers between devices with their start and end apart: 5 -> 6, of which waited for: 3 -> 4; matrix products, arithmetic and copies ran while one was open for 1% -> 1% of each run, Pallas kernels for 0% -> 0%
where the time goes in v1:
time: 218 us; the launch traced here: 217 us
  blocking collectives  92.3 us (42%)
  waiting for transfers between devices  62.4 us (29%)
  starting transfers between devices  40.6 us (19%)
  local copies, waits for them, and re-layouts  8.98 us (4%)
  matrix products  6.75 us (3%)
  other arithmetic  4.76 us (2%)
    all_to_all x1, blocking collectives, sent_to_all(): lax.all_to_all(jnp.broadcast_to(shard[None], (count, *shard.shape)), axis...  56.8 us
    all_to_all x1, waiting for transfers between devices, all_blocks(): lax.all_to_all(jnp.stack([pieces] * lax.axis_size(axes[k])), axes[k], 0, 0)  38.2 us
    all_to_all x1, blocking collectives, sent_and_summed(): pieces = lax.all_to_all(split_up(shard, dim, count), axis, 0, 0, tiled=True)  26.5 us
    all_to_all x1, waiting for transfers between devices, sent_and_summed(): pieces = lax.all_to_all(split_up(shard, dim, count), axis, 0, 0, tiled=True)  20.9 us
    all_to_all x1, starting transfers between devices, all_blocks(): lax.all_to_all(jnp.stack([pieces] * lax.axis_size(axes[k])), axes[k], 0, 0)  14.9 us
    ppermute x2, starting transfers between devices, swapped(): lax.ppermute(shard, axis, [(i, i ^ 1 << stride) for i in range(lax.axis_s...  12.8 us
    all_to_all x1, blocking collectives, all_blocks(): lax.all_to_all(jnp.stack([pieces] * lax.axis_size(axes[k])), axes[k], 0, 0)  9.06 us
    all_to_all x1, starting transfers between devices, sent_and_summed(): pieces = lax.all_to_all(split_up(shard, dim, count), axis, 0, 0, tiled=True)  8.35 us
  transfers between devices with their start and end apart: 6, of which 4 were waited for; matrix products, arithmetic and copies ran while one was open for 1% of the time, Pallas kernels for 0%

profile of v1, /device:TPU:1, one launch (start us, length us, event | category | flops | bytes accessed | tf_op | source)
XLA Modules:
  0.0 217.3 jit_solution(11187432214534088455)
XLA Ops:
  0.6 0.0 copy-start
  0.7 0.8 dynamic-slice_bitcast_fusion
  1.5 9.1 %all_to_all.25 = bf16[4,1,2,3584]{3,2,1,0:T(2,128)(2,1)S(1)} all-to-all(bf16[4,1,2,3584]{3,2,1,0:T(2,128)(2,1)S(1)} %stack.6), channel_id=1, replica_groups=mesh['layer'=8,'latent_0'=4,'latent_1'=16] {'latent_0'}, dimensions={0} | all-to-all | bytes 114688 | tf_op jit(solution)/shard_map/all_to_all | solution.py:20
  10.6 1.4 stack.7
  12.0 14.9 %all-to-all-start.1 = ((bf16[16,4,2,3584]{3,2,1,0:T(2,128)(2,1)}), bf16[16,4,2,3584]{3,2,1,0:T(2,128)(2,1)S(1)}, u32[]{:S(2)}, u32[]{:S(2)}) async-start(bf16[16,4,2,3584]{3,2,1,0:T(2,128)(2,1)} %stack.7), calls=%async_computation.1 | async-start | bytes 1835008 | tf_op jit(solution)/shard_map/all_to_all | solution.py:20
  26.9 1.3 compare_reduce_fusion
  28.9 38.2 %all-to-all-done.1 = bf16[16,4,2,3584]{3,2,1,0:T(2,128)(2,1)S(1)} async-done(((bf16[16,4,2,3584]{3,2,1,0:T(2,128)(2,1)}), bf16[16,4,2,3584]{3,2,1,0:T(2,128)(2,1)S(1)}, u32[]{:S(2)}, u32[]{:S(2)}) %all-to-all-start.1) | async-done | bytes 917536 | tf_op jit(solution)/shard_map/all_to_all | solution.py:20
  67.1 0.0 copy-start.3
  67.1 0.6 copy.19
  67.7 0.3 reshape_reshape.3
  68.1 0.0 copy-start.1
  68.1 0.0 copy-done
  68.1 0.0 copy-done.3
  68.1 0.4 fusion.2
  68.6 6.4 %collective-permute-start = (bf16[128,128]{0,1:T(8,128)(2,1)S(1)}, bf16[128,128]{0,1:T(8,128)(2,1)S(1)}, u32[]{:S(2)}, u32[]{:S(2)}) collective-permute-start(bf16[128,128]{0,1:T(8,128)(2,1)S(1)} %fusion.2), channel_id=1, source_target_pairs={{0,64},{64,0},{128,192},{192,128},{256,320},{320,256},{384,448},{4... | collective-permute-start | bytes 98312 | tf_op jit(solution)/shard_map/ppermute | solution.py:33
  75.0 0.0 copy-done.1
  75.0 1.0 fusion.17
  76.0 0.0 collective-permute-done
  76.1 1.5 fusion.8
  77.6 0.3 fusion.7
  77.9 0.2 pad_maximum_fusion
  78.1 26.5 %all_to_all.26 = f32[4,32,3584]{2,1,0:T(8,128)} all-to-all(f32[4,32,3584]{2,1,0:T(8,128)S(1)} %bitcast.38), channel_id=1, replica_groups=mesh['layer'=8,'latent_0'=4,'latent_1'=16] {'latent_0'}, dimensions={0} | all-to-all | bytes 3670016 | tf_op jit(solution)/shard_map/all_to_all | solution.py:44
  104.5 1.6 reduce_sum.27
  106.2 1.0 reshape.45
  107.2 8.4 %all-to-all-start.3 = ((f32[16,2,3584]{2,1,0:T(2,128)}), f32[16,2,3584]{2,1,0:T(2,128)S(1)}, u32[]{:S(2)}, u32[]{:S(2)}) async-start(f32[16,2,3584]{2,1,0:T(2,128)} %reshape.45), calls=%async_computation.3 | async-start | bytes 917504 | tf_op jit(solution)/shard_map/all_to_all | solution.py:44
  115.6 20.9 %all-to-all-done.3 = f32[16,2,3584]{2,1,0:T(2,128)S(1)} async-done(((f32[16,2,3584]{2,1,0:T(2,128)}), f32[16,2,3584]{2,1,0:T(2,128)S(1)}, u32[]{:S(2)}, u32[]{:S(2)}) %all-to-all-start.3) | async-done | bytes 458784 | tf_op jit(solution)/shard_map/all_to_all | solution.py:44
  136.5 0.1 reduce_sum.28
  136.6 3.2 %collective-permute-start.1 = (f32[2,1792]{1,0:T(2,128)S(1)}, f32[2,1792]{1,0:T(2,128)S(1)}, u32[]{:S(2)}, u32[]{:S(2)}) collective-permute-start(f32[2,1792]{1,0:T(2,128)S(1)} %get-tuple-element.12), channel_id=1, source_target_pairs={{0,128},{64,192},{128,256},{192,320},{256,384},{320,448},{1,129},{... | collective-permute-start | bytes 43016 | tf_op jit(solution)/shard_map/ppermute | solution.py:56
  139.8 1.3 collective-permute-start.2
  141.1 0.8 dynamic-slice_convert_fusion
  141.9 0.0 collective-permute-done.1
  142.0 2.3 %collective-permute-done.2 = f32[2,1792]{1,0:T(2,128)S(1)} collective-permute-done((f32[2,1792]{1,0:T(2,128)S(1)}, f32[2,1792]{1,0:T(2,128)S(1)}, u32[]{:S(2)}, u32[]{:S(2)}) %collective-permute-start.2) | collective-permute-done | bytes 14368 | tf_op jit(solution)/shard_map/ppermute | solution.py:56
  144.3 0.0 copy-start.2
  144.4 0.5 broadcast_in_dim.17
  144.8 56.8 %all_to_all.27 = bf16[64,2,3584]{2,1,0:T(2,128)(2,1)} all-to-all(bf16[64,2,3584]{2,1,0:T(2,128)(2,1)S(1)} %broadcast_in_dim.17), channel_id=1, replica_groups=mesh['layer'=8,'latent_0'=4,'latent_1'=16] {'latent_0','latent_1'}, dimensions={0} | all-to-all | bytes 1835008 | tf_op jit(solution)/shard_map/all_to_all | solution.py:61
  201.6 3.2 %reshape.46 = bf16[128,3584]{1,0:T(8,128)(2,1)} reshape(bf16[64,2,3584]{2,1,0:T(2,128)(2,1)} %all_to_all.27) | data formatting | bytes 1835008 | tf_op jit(solution)/shard_map/reshape | solution.py:13
  204.8 0.0 copy-done.2
  204.8 1.7 fusion.5
  206.5 1.4 convolution_add_fusion
  208.0 6.4 %collective-permute-start.3 = (f32[128,128]{0,1:T(8,128)S(1)}, f32[128,128]{0,1:T(8,128)S(1)}, u32[]{:S(2)}, u32[]{:S(2)}) collective-permute-start(f32[128,128]{0,1:T(8,128)S(1)} %slice_select_fusion), channel_id=1, source_target_pairs={{0,64},{64,0},{128,192},{192,128},{256,320},{320,256},{384,448},{4... | collective-permute-start | bytes 196616 | tf_op jit(solution)/shard_map/ppermute | solution.py:33
  214.4 0.9 collective-permute-done.3
  215.3 0.6 fusion.16
  215.9 1.4 fusion
  (6 shorter events, 0.1 us)
Async XLA Ops:
  0.6 67.5 %copy-start = (bf16[1,3584,128]{2,1,0:T(8,128)(2,1)S(1)}, bf16[1,3584,128]{2,1,0:T(8,128)(2,1)}, u32[]{:S(2)}) copy-start(bf16[1,3584,128]{2,1,0:T(8,128)(2,1)} %param.8) | copy-start | bytes 2752516
  12.0 55.1 %all-to-all-start.1 = ((bf16[16,4,2,3584]{3,2,1,0:T(2,128)(2,1)}), bf16[16,4,2,3584]{3,2,1,0:T(2,128)(2,1)S(1)}, u32[]{:S(2)}, u32[]{:S(2)}) async-start(bf16[16,4,2,3584]{3,2,1,0:T(2,128)(2,1)} %stack.7), calls=%async_computation.1 | async-start | bytes 1835008 | tf_op jit(solution)/shard_map/all_to_all | solution.py:20
  67.1 1.0 copy-start.3
  68.1 6.9 %copy-start.1 = (bf16[1,2,2,128,1792]{4,3,2,1,0:T(8,128)(2,1)S(1)}, bf16[1,2,2,128,1792]{4,3,2,1,0:T(8,128)(2,1)}, u32[]{:S(2)}) copy-start(bf16[1,2,2,128,1792]{4,3,2,1,0:T(8,128)(2,1)} %param.10) | copy-start | bytes 5505028
  68.6 7.5 %collective-permute-start = (bf16[128,128]{0,1:T(8,128)(2,1)S(1)}, bf16[128,128]{0,1:T(8,128)(2,1)S(1)}, u32[]{:S(2)}, u32[]{:S(2)}) collective-permute-start(bf16[128,128]{0,1:T(8,128)(2,1)S(1)} %fusion.2), channel_id=1, source_target_pairs={{0,64},{64,0},{128,192},{192,128},{256,320},{320,256},{384,448},{4... | collective-permute-start | bytes 98312 | tf_op jit(solution)/shard_map/ppermute | solution.py:33
  107.2 29.3 %all-to-all-start.3 = ((f32[16,2,3584]{2,1,0:T(2,128)}), f32[16,2,3584]{2,1,0:T(2,128)S(1)}, u32[]{:S(2)}, u32[]{:S(2)}) async-start(f32[16,2,3584]{2,1,0:T(2,128)} %reshape.45), calls=%async_computation.3 | async-start | bytes 917504 | tf_op jit(solution)/shard_map/all_to_all | solution.py:44
  136.6 5.3 %collective-permute-start.1 = (f32[2,1792]{1,0:T(2,128)S(1)}, f32[2,1792]{1,0:T(2,128)S(1)}, u32[]{:S(2)}, u32[]{:S(2)}) collective-permute-start(f32[2,1792]{1,0:T(2,128)S(1)} %get-tuple-element.12), channel_id=1, source_target_pairs={{0,128},{64,192},{128,256},{192,320},{256,384},{320,448},{1,129},{... | collective-permute-start | bytes 43016 | tf_op jit(solution)/shard_map/ppermute | solution.py:56
  139.8 4.5 %collective-permute-start.2 = (f32[2,1792]{1,0:T(2,128)S(1)}, f32[2,1792]{1,0:T(2,128)S(1)}, u32[]{:S(2)}, u32[]{:S(2)}) collective-permute-start(f32[2,1792]{1,0:T(2,128)S(1)} %get-tuple-element.11), channel_id=1, source_target_pairs={{128,0},{192,64},{256,128},{320,192},{384,256},{448,320},{129,1},{... | collective-permute-start | bytes 43016 | tf_op jit(solution)/shard_map/ppermute | solution.py:56
  144.3 60.5 %copy-start.2 = (bf16[2,1792]{1,0:T(2,128)(2,1)}, bf16[2,1792]{1,0:T(2,128)(2,1)S(1)}, u32[]{:S(2)}) copy-start(bf16[2,1792]{1,0:T(2,128)(2,1)S(1)} %get-tuple-element.10) | copy-start | bytes 21508
  208.0 7.3 %collective-permute-start.3 = (f32[128,128]{0,1:T(8,128)S(1)}, f32[128,128]{0,1:T(8,128)S(1)}, u32[]{:S(2)}, u32[]{:S(2)}) collective-permute-start(f32[128,128]{0,1:T(8,128)S(1)} %slice_select_fusion), channel_id=1, source_target_pairs={{0,64},{64,0},{128,192},{192,128},{256,320},{320,256},{384,448},{4... | collective-permute-start | bytes 196616 | tf_op jit(solution)/shard_map/ppermute | solution.py:33
